TPU v7x, 512 devices: a whole 4x4x16 slice. The times are simulated.
512 devices in a mesh: seq: 128 (over y, z, core), tp: 4 (over x).
Axes of the slice: x: 4, y: 4, z: 16, core: 2. Of those that a mesh axis runs over, the one named last changes fastest.
Arguments:
- queries: float32 [16384, 2048], P('seq', 'tp'), may hold values from -6 to 6
- keys: float32 [16384, 2048], P('seq', 'tp'), may hold values from -6 to 6
- values: float32 [16384, 2048], P('seq', 'tp'), may hold values from -6 to 6
- out_weight: float32 [2048, 4096], P('seq', 'tp'), may hold values from -0.125 to 0.125
Outputs:
- mixed: float32 [16384, 4096], P('seq', 'tp')
All inputs are finite; a program needn't handle non-finite values.
Results may differ from a plain program's by a relative error of at most 0.0003.
Values sent between devices are 32-bit elements; how exact they have to be, the bound alone decides.
A program may use at most 128 MiB of HBM per device.

v0:
```python
import jax
import jax.numpy as jnp
from jax import lax
from jax.sharding import PartitionSpec as P

DH = 128


def prefix(part, axis, combine, identity):
    place = lax.axis_index(axis)
    gathered = jax.tree.map(lambda a: lax.all_gather(a, axis), part)
    state = jax.tree.map(lambda a, e: jnp.zeros_like(a) + jnp.asarray(e, a.dtype), part, identity)

    def one(step, state):
        return combine(
            state, jax.tree.map(lambda a: lax.dynamic_index_in_dim(a, step, 0, False), gathered)
        )

    return lax.fori_loop(0, place, one, state)


def features(inputs):
    return jnp.where(inputs > 0, inputs + 1.0, jnp.exp(jnp.minimum(inputs, 0.0)))


def combine(earlier, later):
    return (earlier[0] + later[0], earlier[1] + later[1])


def shards(queries, keys, values, out_weight):
    highest = lax.Precision.HIGHEST
    tok_rows = queries.shape[0]
    heads_here = queries.shape[1] // DH
    phi_queries = features(queries).reshape(tok_rows, heads_here, DH)
    phi_keys = features(keys).reshape(tok_rows, heads_here, DH)
    value_heads = values.reshape(tok_rows, heads_here, DH)
    memory_state = jnp.einsum("shd,she->hde", phi_keys, value_heads, precision=highest)
    key_total = jnp.sum(phi_keys, axis=0)
    identity = (jnp.zeros_like(memory_state), jnp.zeros_like(key_total))
    prior_state, prior_total = prefix((memory_state, key_total), "seq", combine, identity)
    causal_mask = jnp.arange(tok_rows)[:, None] >= jnp.arange(tok_rows)[None, :]
    scores = jnp.einsum("thd,shd->hts", phi_queries, phi_keys, precision=highest)
    scores = jnp.where(causal_mask[None], scores, 0.0)
    numerator = jnp.einsum("hts,shd->thd", scores, value_heads, precision=highest)
    numerator = numerator + jnp.einsum("thd,hde->the", phi_queries, prior_state, precision=highest)
    denominator = jnp.sum(scores, axis=2).T + jnp.einsum(
        "thd,hd->th", phi_queries, prior_total, precision=highest
    )
    attended = (numerator / denominator[:, :, None]).reshape(tok_rows, heads_here * DH)
    every_head = lax.all_gather(attended, "tp", axis=1, tiled=True)
    gathered = lax.all_gather(out_weight, "seq", axis=0, tiled=True)
    mixed = jnp.dot(every_head, gathered, precision=highest, preferred_element_type=jnp.float32)
    return mixed


def solution(mesh):
    return jax.shard_map(
        shards,
        mesh=mesh,
        in_specs=(P("seq", "tp"), P("seq", "tp"), P("seq", "tp"), P("seq", "tp")),
        out_specs=P("seq", "tp"),
        check_vma=False,
    )
```

profile of v0, /device:TPU:1, one launch (start us, length us, event | category | flops | bytes accessed | tf_op | source)
XLA Modules:
  0.0 401.2 jit_solution(6245858117362999715)
XLA Ops:
  6.5 0.0 copy-start
  6.5 0.0 all-gather.9.cloned.1.call-start
  6.5 1.1 fusion.7
  7.6 0.1 copy.31
  7.7 0.0 copy-done
  7.8 1.1 fusion.3
  8.8 0.0 all-gather.9.cloned.1.call-update
  8.9 0.0 all-gather.7.cloned.1.call-start
  8.9 0.7 all-gather.7.cloned.1.call-update
  9.6 0.0 all-gather.5.cloned.1.call-start
  9.7 1.0 exponential_select_fusion.1
  10.7 0.1 copy.30
  10.8 108.5 %all_gather.21 = f32[128,4,128]{2,1,0:T(4,128)S(1)} all-gather(f32[1,4,128]{2,1,0:T(4,128)S(1)} %bitcast.58), channel_id=1, replica_groups=mesh['seq'=128,'tp'=4] {'seq'}, dimensions={0}, use_global_device_ids=true | all-gather | bytes 264192 | tf_op jit(solution)/shard_map/all_gather | solution.py:11
  119.4 0.6 fusion.8
  120.0 0.6 convolution_bitcast_fusion.1
  120.6 90.9 %all-gather.9.cloned.1.call-done = f32[512,128,128]{2,1,0:T(8,128)} async-done(((f32[4,128,128]{2,1,0:T(8,128)}), f32[512,128,128]{2,1,0:T(8,128)}) %all-gather.9.cloned.1.call-update) | async-done | bytes 33554448 | tf_op jit(solution)/shard_map/all_gather | solution.py:11
  211.6 1.1 while.12
  211.6 1.0 bitcast_add_fusion.4
  212.6 0.3 fusion.9
  212.9 1.3 fusion.1
  214.3 0.0 all-gather.5.cloned.1.call-update
  214.3 143.7 %all-gather.7.cloned.1.call-done = f32[2048,1024]{1,0:T(8,128)} async-done(((f32[16,1024]{1,0:T(8,128)}), f32[2048,1024]{1,0:T(8,128)}) %all-gather.7.cloned.1.call-update) | async-done | bytes 8388624 | tf_op jit(solution)/shard_map/all_gather | solution.py:51
  358.0 27.5 %all-gather.5.cloned.1.call-done = f32[128,2048]{0,1:T(8,128)} async-done(((f32[128,512]{0,1:T(8,128)}), f32[128,2048]{0,1:T(8,128)}) %all-gather.5.cloned.1.call-update) | async-done | bytes 1048592 | tf_op jit(solution)/shard_map/all_gather | solution.py:50
  385.5 9.1 %fusion.10 = f32[128,1024]{1,0:T(8,128)} fusion(f32[128,2048]{0,1:T(8,128)} %all-gather.5.cloned.1.call-done, f32[2048,1024]{1,0:T(8,128)} %all-gather.7.cloned.1.call-done), kind=kOutput, calls=%fused_computation.19 | convolution fusion | flops 3221225472 | bytes 9961472 | tf_op jit(solution)/shard_map/dot_general | solution.py:52
  (5 shorter events, 0.1 us)
Async XLA Ops:
  6.5 1.2 copy-start
  6.5 205.0 %all-gather.9.cloned.1.call-start = ((), (), s32[]{:S(2)}) async-start(), calls=%async_computation.2 | async-start | bytes 33816576 | tf_op jit(solution)/shard_map/all_gather | solution.py:11
  8.9 349.1 %all-gather.7.cloned.1.call-start = ((), (), s32[]{:S(2)}) async-start(), calls=%async_computation.1 | async-start | bytes 8454144 | tf_op jit(solution)/shard_map/all_gather | solution.py:51
  9.6 375.9 %all-gather.5.cloned.1.call-start = ((), (), s32[]{:S(2)}) async-start(), calls=%async_computation | async-start | bytes 1310720 | tf_op jit(solution)/shard_map/all_gather | solution.py:50
Sparse Core Ops, SparseCore 0:
  10.5 200.9 all-gather.8
  214.7 143.2 all-gather.6
  360.1 25.3 all-gather.4
where the time goes:
time: 405 us; the launch traced here: 401 us
  waiting for transfers between devices  263 us (65%)
  blocking collectives  109 us (27%)
  between operations  13.2 us (3%)
  matrix products  13.1 us (3%)
    all_gather x1, waiting for transfers between devices, shards(): gathered = lax.all_gather(out_weight, 'seq', axis=0, tiled=True)  144 us
    all_gather x1, blocking collectives, prefix(): gathered = jax.tree.map(lambda a: lax.all_gather(a, axis), part)  109 us
    all_gather x1, waiting for transfers between devices, prefix(): gathered = jax.tree.map(lambda a: lax.all_gather(a, axis), part)  90.9 us
    all_gather x1, waiting for transfers between devices, shards(): every_head = lax.all_gather(attended, 'tp', axis=1, tiled=True)  27.5 us
    dot_general x1, matrix products, shards(): jnp.dot(every_head, gathered, precision=highest, preferred_element_type=j...  9.14 us
  transfers between devices with their start and end apart: 3, of which 3 were waited for; matrix products, arithmetic and copies ran while one was open for 1% of the time, Pallas kernels for 0%

commit v1 on v0

--- a/solution.py
+++ b/solution.py
@@ -4,6 +4,13 @@
 from jax.sharding import PartitionSpec as P
 
 DH = 128
+
+
+def gather_over(shard, axis, d):
+    count = lax.axis_size(axis)
+    blocks = jnp.stack([shard for _ in range(count)])
+    blocks = lax.all_to_all(blocks, axis, split_axis=0, concat_axis=0)
+    return jnp.concatenate(blocks, axis=d)
 
 
 def prefix(part, axis, combine, identity):
@@ -48,7 +55,7 @@
     )
     attended = (numerator / denominator[:, :, None]).reshape(tok_rows, heads_here * DH)
     every_head = lax.all_gather(attended, "tp", axis=1, tiled=True)
-    gathered = lax.all_gather(out_weight, "seq", axis=0, tiled=True)
+    gathered = gather_over(out_weight, "seq", 0)
     mixed = jnp.dot(every_head, gathered, precision=highest, preferred_element_type=jnp.float32)
     return mixed
 

time: 405 us -> 752 us (1.86)
  blocking collectives: 109 us -> 538 us
  waiting for transfers between devices: 263 us -> 154 us
  starting transfers between devices: 0.08 us -> 21.2 us
    all_gather x1, blocking collectives: 109 us -> 538 us  [prefix(): gathered = jax.tree.map(lambda a: lax.all_gather(a, axis), part)]
    all_gather x1 -> x0, waiting for transfers between devices: 144 us -> none  [shards(): gathered = lax.all_gather(out_weight, 'seq', axis=0, tiled=True)]
    all_gather x1, waiting for transfers between devices: 27.5 us -> 154 us  [shards(): every_head = lax.all_gather(attended, 'tp', axis=1, tiled=True)]
    all_gather x1, waiting for transfers between devices: 90.9 us -> 0.02 us  [prefix(): gathered = jax.tree.map(lambda a: lax.all_gather(a, axis), part)]
    all_to_all x0 -> x1, starting transfers between devices: none -> 21.2 us  [gather_over(): blocks = lax.all_to_all(blocks, axis, split_axis=0, concat_axis=0)]
  transfers between devices with their start and end apart: 3 -> 3, of which waited for: 3 -> 1; matrix products, arithmetic and copies ran while one was open for 1% -> 1% of each run, Pallas kernels for 0% -> 0%
where the time goes in v1:
time: 752 us; the launch traced here: 747 us
  blocking collectives  538 us (72%)
  waiting for transfers between devices  154 us (20%)
  starting transfers between devices  21.2 us (3%)
  between operations  13.5 us (2%)
  matrix products  13.1 us (2%)
    all_gather x1, blocking collectives, prefix(): gathered = jax.tree.map(lambda a: lax.all_gather(a, axis), part)  538 us
    all_gather x1, waiting for transfers between devices, shards(): every_head = lax.all_gather(attended, 'tp', axis=1, tiled=True)  154 us
    all_to_all x1, starting transfers between devices, gather_over(): blocks = lax.all_to_all(blocks, axis, split_axis=0, concat_axis=0)  21.2 us
  transfers between devices with their start and end apart: 3, of which 1 were waited for; matrix products, arithmetic and copies ran while one was open for 1% of the time, Pallas kernels for 0%

profile of v1, /device:TPU:1, one launch (start us, length us, event | category | flops | bytes accessed | tf_op | source)
XLA Modules:
  0.0 747.4 jit_solution(8074428069715510336)
XLA Ops:
  6.5 0.0 copy-start
  6.5 0.0 all-gather.6.cloned.1.call-start
  6.5 1.1 fusion.7
  7.6 0.1 copy.31
  7.7 0.0 copy-done
  7.8 1.1 fusion.3
  8.8 0.0 all-gather.6.cloned.1.call-update
  8.9 5.1 stack.2
  14.0 0.0 copy-start.1
  14.0 21.2 %all-to-all-start = ((f32[128,16,1024]{2,1,0:T(8,128)}), f32[128,16,1024]{2,1,0:T(8,128)}, u32[]{:S(2)}, u32[]{:S(2)}) async-start(f32[128,16,1024]{2,1,0:T(8,128)} %stack.2), calls=%async_computation | async-start | bytes 16777216 | tf_op jit(solution)/shard_map/all_to_all | solution.py:12
  35.1 0.0 all-gather.4.cloned.1.call-start
  35.2 0.0 copy-done.1
  35.2 0.1 exponential_select_fusion.1
  35.3 0.1 copy.30
  35.4 537.6 %all_gather.18 = f32[128,4,128]{2,1,0:T(4,128)S(1)} all-gather(f32[1,4,128]{2,1,0:T(4,128)S(1)} %bitcast.59), channel_id=1, replica_groups=mesh['seq'=128,'tp'=4] {'seq'}, dimensions={0}, use_global_device_ids=true | all-gather | bytes 264192 | tf_op jit(solution)/shard_map/all_gather | solution.py:18
  573.0 0.6 fusion.8
  573.6 0.6 convolution_bitcast_fusion.1
  574.2 0.0 all-gather.6.cloned.1.call-done
  574.3 1.1 while.12
  574.3 1.0 bitcast_add_fusion.4
  575.4 0.3 fusion.9
  575.7 1.3 fusion.1
  577.0 0.0 all-gather.4.cloned.1.call-update
  577.0 0.0 all-to-all-done
  577.0 154.4 %all-gather.4.cloned.1.call-done = f32[128,2048]{0,1:T(8,128)} async-done(((f32[128,512]{0,1:T(8,128)}), f32[128,2048]{0,1:T(8,128)}) %all-gather.4.cloned.1.call-update) | async-done | bytes 1048592 | tf_op jit(solution)/shard_map/all_gather | solution.py:57
  731.4 9.1 %fusion.10 = f32[128,1024]{1,0:T(8,128)} fusion(f32[128,2048]{0,1:T(8,128)} %all-gather.4.cloned.1.call-done, f32[2048,1024]{1,0:T(8,128)} %bitcast.12), kind=kOutput, calls=%fused_computation.19 | convolution fusion | flops 3221225472 | bytes 9961472 | tf_op jit(solution)/shard_map/dot_general | solution.py:59
  (5 shorter events, 0.1 us)
Async XLA Ops:
  6.5 1.2 copy-start
  6.5 567.7 %all-gather.6.cloned.1.call-start = ((), (), s32[]{:S(2)}) async-start(), calls=%async_computation.2 | async-start | bytes 33816576 | tf_op jit(solution)/shard_map/all_gather | solution.py:18
  14.0 21.2 %copy-start.1 = (f32[128,512]{1,0:T(8,128)S(1)}, f32[128,512]{1,0:T(8,128)}, u32[]{:S(2)}) copy-start(f32[128,512]{1,0:T(8,128)} %param.6) | copy-start | bytes 786436
  14.0 563.0 %all-to-all-start = ((f32[128,16,1024]{2,1,0:T(8,128)}), f32[128,16,1024]{2,1,0:T(8,128)}, u32[]{:S(2)}, u32[]{:S(2)}) async-start(f32[128,16,1024]{2,1,0:T(8,128)} %stack.2), calls=%async_computation | async-start | bytes 16777216 | tf_op jit(solution)/shard_map/all_to_all | solution.py:12
  35.1 696.2 %all-gather.4.cloned.1.call-start = ((), (), s32[]{:S(2)}) async-start(), calls=%async_computation.1 | async-start | bytes 1310720 | tf_op jit(solution)/shard_map/all_gather | solution.py:57
Sparse Core Ops, SparseCore 0:
  10.5 494.6 all-gather.5
  577.1 154.1 all-gather.3

commit v2 on v0

--- a/solution.py
+++ b/solution.py
@@ -47,7 +47,25 @@
         "thd,hd->th", phi_queries, prior_total, precision=highest
     )
     attended = (numerator / denominator[:, :, None]).reshape(tok_rows, heads_here * DH)
-    every_head = lax.all_gather(attended, "tp", axis=1, tiled=True)
+    size, index, rows = (lax.axis_size("tp"), lax.axis_index("tp"), attended.shape[1])
+    upward = [(i, (i + 1) % size) for i in range(size)]
+    left = [(i, (i - 1) % size) for i in range(size)]
+    every_head = jnp.zeros(
+        (*attended.shape[:1], size * rows, *attended.shape[1 + 1 :]), attended.dtype
+    )
+    every_head = lax.dynamic_update_slice_in_dim(every_head, attended, index * rows, axis=1)
+    from_left = from_right = attended
+    middle = size // 2
+    for k in range(1, middle + 1):
+        from_left = lax.ppermute(from_left, "tp", upward)
+        every_head = lax.dynamic_update_slice_in_dim(
+            every_head, from_left, (index - k) % size * rows, axis=1
+        )
+        if k < size - middle:
+            from_right = lax.ppermute(from_right, "tp", left)
+            every_head = lax.dynamic_update_slice_in_dim(
+                every_head, from_right, (index + k) % size * rows, axis=1
+            )
     gathered = lax.all_gather(out_weight, "seq", axis=0, tiled=True)
     mixed = jnp.dot(every_head, gathered, precision=highest, preferred_element_type=jnp.float32)
     return mixed

time: 405 us -> 377 us (0.931)
  waiting for transfers between devices: 263 us -> 227 us
  starting transfers between devices: 0.08 us -> 8.71 us
    all_gather x1 -> x0, waiting for transfers between devices: 27.5 us -> none  [shards(): every_head = lax.all_gather(attended, 'tp', axis=1, tiled=True)]
    all_gather x1, waiting for transfers between devices: 144 us -> 123 us  [shards(): gathered = lax.all_gather(out_weight, 'seq', axis=0, tiled=True)]
    ppermute x0 -> x3, waiting for transfers between devices: none -> 12.5 us  [the longest x2 12.4 us: shards(): from_left = lax.ppermute(from_left, 'tp', upward)]
    ppermute x0 -> x3, starting transfers between devices: none -> 8.66 us  [the longest x2 5.27 us: shards(): from_left = lax.ppermute(from_left, 'tp', upward)]
  transfers between devices with their start and end apart: 3 -> 5, of which waited for: 3 -> 5; matrix products, arithmetic and copies ran while one was open for 1% -> 1% of each run, Pallas kernels for 0% -> 0%
where the time goes in v2:
time: 377 us; the launch traced here: 373 us
  waiting for transfers between devices  227 us (60%)
  blocking collectives  109 us (29%)
  between operations  13.6 us (4%)
  matrix products  11 us (3%)
  starting transfers between devices  8.71 us (2%)
    all_gather x1, waiting for transfers between devices, shards(): gathered = lax.all_gather(out_weight, 'seq', axis=0, tiled=True)  123 us
    all_gather x1, blocking collectives, prefix(): gathered = jax.tree.map(lambda a: lax.all_gather(a, axis), part)  109 us
    all_gather x1, waiting for transfers between devices, prefix(): gathered = jax.tree.map(lambda a: lax.all_gather(a, axis), part)  91.2 us
    ppermute x2, waiting for transfers between devices, shards(): from_left = lax.ppermute(from_left, 'tp', upward)  12.4 us
    dot_general x1, matrix products, shards(): jnp.dot(every_head, gathered, precision=highest, preferred_element_type=j...  7.79 us
  transfers between devices with their start and end apart: 5, of which 5 were waited for; matrix products, arithmetic and copies ran while one was open for 1% of the time, Pallas kernels for 0%

profile of v2, /device:TPU:1, one launch (start us, length us, event | category | flops | bytes accessed | tf_op | source)
XLA Modules:
  0.0 372.9 jit_solution(12443284118268577519)
XLA Ops:
  6.5 0.0 copy-start
  6.5 0.0 all-gather.6.cloned.1.call-start
  6.5 1.1 fusion.7
  7.6 0.1 copy.31
  7.7 0.0 copy-done
  7.8 1.1 fusion.3
  8.8 0.0 all-gather.6.cloned.1.call-update
  8.9 0.0 all-gather.4.cloned.1.call-start
  8.9 0.7 all-gather.4.cloned.1.call-update
  9.6 1.0 exponential_select_fusion.1
  10.6 0.1 copy.30
  10.8 108.6 %all_gather.18 = f32[128,4,128]{2,1,0:T(4,128)S(1)} all-gather(f32[1,4,128]{2,1,0:T(4,128)S(1)} %bitcast.60), channel_id=1, replica_groups=mesh['seq'=128,'tp'=4] {'seq'}, dimensions={0}, use_global_device_ids=true | all-gather | bytes 264192 | tf_op jit(solution)/shard_map/all_gather | solution.py:11
  119.3 0.6 fusion.8
  120.0 0.6 convolution_bitcast_fusion.1
  120.6 91.2 %all-gather.6.cloned.1.call-done = f32[512,128,128]{2,1,0:T(8,128)} async-done(((f32[4,128,128]{2,1,0:T(8,128)}), f32[512,128,128]{2,1,0:T(8,128)}) %all-gather.6.cloned.1.call-update) | async-done | bytes 33554448 | tf_op jit(solution)/shard_map/all_gather | solution.py:11
  211.8 1.1 while.12
  211.8 1.0 bitcast_add_fusion.4
  212.9 0.3 fusion.9
  213.2 0.6 fusion.1
  213.8 3.1 collective-permute-start
  216.9 3.4 collective-permute-start.1
  220.4 4.2 %collective-permute-done = f32[128,512]{0,1:T(8,128)S(1)} collective-permute-done((f32[128,512]{0,1:T(8,128)S(1)}, f32[128,512]{0,1:T(8,128)S(1)}, u32[]{:S(2)}, u32[]{:S(2)}) %collective-permute-start) | collective-permute-done | bytes 262176 | tf_op jit(solution)/shard_map/ppermute | solution.py:60
  224.6 2.2 collective-permute-start.2
  226.8 0.1 broadcast_in_dim.23
  226.9 0.1 collective-permute-done.1
  227.0 8.2 %collective-permute-done.2 = f32[128,512]{0,1:T(8,128)S(1)} collective-permute-done((f32[128,512]{0,1:T(8,128)S(1)}, f32[128,512]{0,1:T(8,128)S(1)}, u32[]{:S(2)}, u32[]{:S(2)}) %collective-permute-start.2) | collective-permute-done | bytes 262176 | tf_op jit(solution)/shard_map/ppermute | solution.py:60
  235.3 123.0 %all-gather.4.cloned.1.call-done = f32[2048,1024]{1,0:T(8,128)} async-done(((f32[16,1024]{1,0:T(8,128)}), f32[2048,1024]{1,0:T(8,128)}) %all-gather.4.cloned.1.call-update) | async-done | bytes 8388624 | tf_op jit(solution)/shard_map/all_gather | solution.py:69
  358.3 7.8 %fusion.10 = f32[128,1024]{1,0:T(8,128)} fusion(f32[128,2048]{0,1:T(8,128)S(1)} %constant_dynamic-update-slice_fusion, f32[2048,1024]{1,0:T(8,128)} %all-gather.4.cloned.1.call-done), kind=kOutput, calls=%fused_computation.23 | convolution fusion | flops 3221225472 | bytes 9961472 | tf_op jit(solution)/shard_map/dot_general | solution.py:70
  (9 shorter events, 0.2 us)
Async XLA Ops:
  6.5 1.2 copy-start
  6.5 205.2 %all-gather.6.cloned.1.call-start = ((), (), s32[]{:S(2)}) async-start(), calls=%async_computation.1 | async-start | bytes 33816576 | tf_op jit(solution)/shard_map/all_gather | solution.py:11
  8.9 349.4 %all-gather.4.cloned.1.call-start = ((), (), s32[]{:S(2)}) async-start(), calls=%async_computation | async-start | bytes 8454144 | tf_op jit(solution)/shard_map/all_gather | solution.py:69
  213.8 10.8 %collective-permute-start = (f32[128,512]{0,1:T(8,128)S(1)}, f32[128,512]{0,1:T(8,128)S(1)}, u32[]{:S(2)}, u32[]{:S(2)}) collective-permute-start(f32[128,512]{0,1:T(8,128)S(1)} %bitcast.55), channel_id=1, source_target_pairs={{0,1},{1,2},{2,3},{3,0},{4,5},{5,6},{6,7},{7,4},{8,9},{9,10},{10,1... | collective-permute-start | bytes 786440 | tf_op jit(solution)/shard_map/ppermute | solution.py:60
  216.9 10.1 %collective-permute-start.1 = (f32[128,512]{0,1:T(8,128)S(1)}, f32[128,512]{0,1:T(8,128)S(1)}, u32[]{:S(2)}, u32[]{:S(2)}) collective-permute-start(f32[128,512]{0,1:T(8,128)S(1)} %bitcast.56), channel_id=1, source_target_pairs={{0,3},{1,0},{2,1},{3,2},{4,7},{5,4},{6,5},{7,6},{8,11},{9,8},{10,9... | collective-permute-start | bytes 786440 | tf_op jit(solution)/shard_map/ppermute | solution.py:65
  224.6 10.6 %collective-permute-start.2 = (f32[128,512]{0,1:T(8,128)S(1)}, f32[128,512]{0,1:T(8,128)S(1)}, u32[]{:S(2)}, u32[]{:S(2)}) collective-permute-start(f32[128,512]{0,1:T(8,128)S(1)} %collective-permute-done), channel_id=1, source_target_pairs={{0,1},{1,2},{2,3},{3,0},{4,5},{5,6},{6,7},{7,4},{8,9},{9,10},{10,1... | collective-permute-start | bytes 786440 | tf_op jit(solution)/shard_map/ppermute | solution.py:60
Sparse Core Ops, SparseCore 0:
  10.5 201.2 all-gather.5
  214.9 143.2 all-gather.3
